TPU v7x, 32 devices: a whole 2x2x4 slice. The times are simulated.
32 devices in a mesh: fsdp: 16 (over z, y, core), dp: 2 (over x).
Axes of the slice: x: 2, y: 2, z: 4, core: 2. Of those that a mesh axis runs over, the one named last changes fastest.
Arguments:
- tokens: bfloat16 [32768, 1024], P(('fsdp', 'dp')), may hold values from -6 to 6
- item_start: int32 [32768], P(('fsdp', 'dp')), may hold values from 0 to 896, as said below
- out_grad: bfloat16 [32768, 1024], P(('fsdp', 'dp')), may hold values from -6 to 6
- norm_gains: float32 [2, 1024], replicated, may hold values from 0.5 to 1.5
- norm_shifts: float32 [2, 1024], replicated, may hold values from -1.25 to 1.25
- w_qkv: bfloat16 [1024, 3072], P('fsdp'), may hold values from -0.1875 to 0.1875
- bias_qkv: float32 [3072], replicated, may hold values from -1.25 to 1.25
- w_out: bfloat16 [1024, 1024], P('fsdp'), may hold values from -0.5 to 0.5
- w_fc: bfloat16 [1024, 4096], P('fsdp'), may hold values from -0.1875 to 0.1875
- bias_fc: float32 [4096], replicated, may hold values from -1.75 to 1.75
- w_proj: bfloat16 [4096, 1024], P('fsdp'), may hold values from -0.09375 to 0.09375
- out_biases: float32 [2, 1024], replicated, may hold values from -1.25 to 1.25
- adapters: float32 [4, 1024, 4], replicated, may hold values from -0.3125 to 0.3125
- momentum: float32 [4, 1024, 4], replicated, may hold values from -1280 to 1280
- average: float32 [4, 1024, 4], replicated, may hold values from -0.3125 to 0.3125
Outputs:
- block_out: bfloat16 [32768, 1024], P(('fsdp', 'dp'))
- in_grad: float32 [32768, 1024], P(('fsdp', 'dp'))
- adapter_grad: float32 [4, 1024, 4], replicated
- new_momentum: float32 [4, 1024, 4], replicated
- new_adapters: float32 [4, 1024, 4], replicated
- new_average: float32 [4, 1024, 4], replicated
- adapter_copy: bfloat16 [4, 1024, 4], replicated
Inputs may be any that keep to these rules, and one draw needn't show every extreme that they name: `item_start`: each device's 1024 rows are cut into aligned runs of 1024 rows, and each run into items of 1024, 512, 256 or 128 rows at aligned places; every row holds the first row of its item, counted within its device. Every draw has an item of 1024 rows and one of 128 rows.
All inputs are finite; a program needn't handle non-finite values.
Results may differ from a plain program's by a relative error of at most 0.014.
The roundings to bfloat16 on the way count: a program that leaves them out, or rounds other values in their place, can miss the bound.
Values may be sent and summed in bfloat16 or wider, within the bound.
A program may use at most 256 MiB of HBM per device.

v0:
```python
import jax
import jax.numpy as jnp
from jax import lax
from jax.sharding import PartitionSpec as P

HEADS = 16
query_span = 512
adapter_scale = 8.0
score_scale = 0.125


def contract_trailing(left, right):
    return lax.dot_general(
        left, right, (((1,), (1,)), ((), ())), preferred_element_type=jnp.float32
    )


def contract_leading(left, right):
    return lax.dot_general(
        left, right, (((0,), (0,)), ((), ())), preferred_element_type=jnp.float32
    )


def layer_norm(values, gain, shift):
    center = values - jnp.mean(values, axis=-1, keepdims=True)
    spread = jnp.mean(center * center, axis=-1, keepdims=True)
    return center * lax.rsqrt(spread + 1e-05) * gain + shift


def gelu_tanh(values):
    return (
        0.5
        * values
        * (1.0 + jnp.tanh(0.7978845608 * (values + 0.044715 * values * values * values)))
    )


def block_scores(query_heads, key_heads, starts, block_index, span_rows):
    row_count = key_heads.shape[0]
    begin_row = block_index * span_rows
    query_block = lax.dynamic_slice_in_dim(query_heads, begin_row, span_rows, 0)
    start_block = lax.dynamic_slice_in_dim(starts, begin_row, span_rows, 0)
    columns = jnp.arange(row_count, dtype=jnp.int32)
    row_ids = begin_row + jnp.arange(span_rows, dtype=jnp.int32)
    scores = (
        jnp.einsum("qhe,khe->hqk", query_block, key_heads, preferred_element_type=jnp.float32)
        * score_scale
    )
    visible = (start_block[:, None] <= columns[None, :]) & (columns[None, :] <= row_ids[:, None])
    return (query_block, jnp.where(visible[None], scores, jnp.float32(-1e30)))


def attend_forward(query_heads, key_heads, value_heads, starts):
    row_count = query_heads.shape[0]
    span_rows = min(query_span, row_count)

    def one_block(block_index):
        query_block, scores = block_scores(query_heads, key_heads, starts, block_index, span_rows)
        highest = jnp.max(scores, axis=-1, keepdims=True)
        raised = jnp.exp(scores - highest)
        totals = jnp.sum(raised, axis=-1, keepdims=True)
        probs = raised / totals
        result = jnp.einsum(
            "hqk,khe->qhe",
            probs.astype(jnp.bfloat16),
            value_heads,
            preferred_element_type=jnp.float32,
        )
        return (result.astype(jnp.bfloat16), (highest + jnp.log(totals))[..., 0])

    outputs, log_sums = lax.map(one_block, jnp.arange(row_count // span_rows, dtype=jnp.int32))
    return (outputs.reshape(query_heads.shape), log_sums)


def attend_backward(query_heads, key_heads, value_heads, grad_heads, log_sums, starts):
    row_count = query_heads.shape[0]
    span_rows = min(query_span, row_count)

    def one_block(carry, block_index):
        grad_keys, value_gradient = carry
        query_block, scores = block_scores(query_heads, key_heads, starts, block_index, span_rows)
        grad_block = lax.dynamic_slice_in_dim(grad_heads, block_index * span_rows, span_rows, 0)
        probs = jnp.exp(scores - log_sums[block_index][:, :, None])
        grad_probs = jnp.einsum(
            "qhe,khe->hqk", grad_block, value_heads, preferred_element_type=jnp.float32
        )
        value_gradient = value_gradient + jnp.einsum(
            "hqk,qhe->khe",
            probs.astype(jnp.bfloat16),
            grad_block,
            preferred_element_type=jnp.float32,
        )
        inner = jnp.sum(probs * grad_probs, axis=-1, keepdims=True)
        grad_scores = (probs * (grad_probs - inner)).astype(jnp.bfloat16)
        query_gradient = (
            jnp.einsum("hqk,khe->qhe", grad_scores, key_heads, preferred_element_type=jnp.float32)
            * score_scale
        )
        grad_keys = (
            grad_keys
            + jnp.einsum(
                "hqk,qhe->khe", grad_scores, query_block, preferred_element_type=jnp.float32
            )
            * score_scale
        )
        return ((grad_keys, value_gradient), query_gradient.astype(jnp.bfloat16))

    zeros_heads = jnp.zeros(key_heads.shape, jnp.float32)
    (grad_keys, value_gradient), grad_queries = lax.scan(
        one_block, (zeros_heads, zeros_heads), jnp.arange(row_count // span_rows, dtype=jnp.int32)
    )
    return (
        grad_queries.reshape(query_heads.shape),
        grad_keys.astype(jnp.bfloat16),
        value_gradient.astype(jnp.bfloat16),
    )


def per_device(
    tokens,
    item_start,
    out_grad,
    norm_gains,
    norm_shifts,
    w_qkv,
    bias_qkv,
    w_out,
    w_fc,
    bias_fc,
    w_proj,
    out_biases,
    adapters,
    momentum,
    average,
):
    row_count, hidden_width = tokens.shape
    head_size = hidden_width // HEADS
    qkv_full, out_full = (
        lax.all_gather(w_qkv, "fsdp", axis=0, tiled=True),
        lax.all_gather(w_out, "fsdp", axis=0, tiled=True),
    )
    fc_full, proj_full = (
        lax.all_gather(w_fc, "fsdp", axis=0, tiled=True),
        lax.all_gather(w_proj, "fsdp", axis=0, tiled=True),
    )
    reduced_adapter_pass = adapters.astype(jnp.bfloat16)
    residual = tokens.astype(jnp.float32)

    def norm_first(values):
        return layer_norm(values, norm_gains[0], norm_shifts[0])

    def norm_second(values):
        return layer_norm(values, norm_gains[1], norm_shifts[1])

    normed_one, back_first = jax.vjp(norm_first, residual)
    normed_one = normed_one.astype(jnp.bfloat16)
    mixed_tokens_full = jnp.dot(normed_one, qkv_full, preferred_element_type=jnp.float32) + bias_qkv
    query_down_matrix = jnp.dot(
        normed_one, reduced_adapter_pass[0], preferred_element_type=jnp.float32
    ).astype(jnp.bfloat16)
    value_down_matrix = jnp.dot(
        normed_one, reduced_adapter_pass[2], preferred_element_type=jnp.float32
    ).astype(jnp.bfloat16)
    query_rows = (
        mixed_tokens_full[:, :hidden_width]
        + adapter_scale * contract_trailing(query_down_matrix, reduced_adapter_pass[1])
    ).astype(jnp.bfloat16)
    keys_all = mixed_tokens_full[:, hidden_width : 2 * hidden_width].astype(jnp.bfloat16)
    value_rows_full = (
        mixed_tokens_full[:, 2 * hidden_width :]
        + adapter_scale * contract_trailing(value_down_matrix, reduced_adapter_pass[3])
    ).astype(jnp.bfloat16)
    heads_shape = (row_count, HEADS, head_size)
    query_heads = query_rows.reshape(heads_shape)
    key_heads = keys_all.reshape(heads_shape)
    value_heads = value_rows_full.reshape(heads_shape)
    attended, log_sums = attend_forward(query_heads, key_heads, value_heads, item_start)
    attended = attended.reshape(row_count, hidden_width)
    middle = (
        residual + jnp.dot(attended, out_full, preferred_element_type=jnp.float32) + out_biases[0]
    )
    normed_two, back_second = jax.vjp(norm_second, middle)
    normed_two = normed_two.astype(jnp.bfloat16)
    pre_act = jnp.dot(normed_two, fc_full, preferred_element_type=jnp.float32) + bias_fc
    activation, back_gelu = jax.vjp(gelu_tanh, pre_act)
    activation = activation.astype(jnp.bfloat16)
    result = (
        middle + jnp.dot(activation, proj_full, preferred_element_type=jnp.float32) + out_biases[1]
    )
    block_out = result.astype(jnp.bfloat16)
    fc_back, proj_back = (
        lax.all_gather(w_fc, "fsdp", axis=0, tiled=True),
        lax.all_gather(w_proj, "fsdp", axis=0, tiled=True),
    )
    qkv_back, out_back = (
        lax.all_gather(w_qkv, "fsdp", axis=0, tiled=True),
        lax.all_gather(w_out, "fsdp", axis=0, tiled=True),
    )
    grad_act = contract_trailing(out_grad, proj_back)
    grad_pre = back_gelu(grad_act)[0].astype(jnp.bfloat16)
    grad_norm_two = contract_trailing(grad_pre, fc_back)
    grad_middle = out_grad.astype(jnp.float32) + back_second(grad_norm_two)[0]
    grad_branch = grad_middle.astype(jnp.bfloat16)
    grad_attended = (
        contract_trailing(grad_branch, out_back).astype(jnp.bfloat16).reshape(heads_shape)
    )
    query_gradient, grad_keys, value_gradient = attend_backward(
        query_heads, key_heads, value_heads, grad_attended, log_sums, item_start
    )
    query_gradient = query_gradient.reshape(row_count, hidden_width)
    grad_keys = grad_keys.reshape(row_count, hidden_width)
    value_gradient = value_gradient.reshape(row_count, hidden_width)
    grad_mixed = jnp.concatenate([query_gradient, grad_keys, value_gradient], axis=1)
    grad_down_q = (
        adapter_scale
        * jnp.dot(query_gradient, reduced_adapter_pass[1], preferred_element_type=jnp.float32)
    ).astype(jnp.bfloat16)
    grad_down_v = (
        adapter_scale
        * jnp.dot(value_gradient, reduced_adapter_pass[3], preferred_element_type=jnp.float32)
    ).astype(jnp.bfloat16)
    grad_norm_one = (
        contract_trailing(grad_mixed, qkv_back)
        + contract_trailing(grad_down_q, reduced_adapter_pass[0])
        + contract_trailing(grad_down_v, reduced_adapter_pass[2])
    )
    in_grad = grad_middle + back_first(grad_norm_one)[0]
    local_grads = jnp.stack(
        [
            contract_leading(normed_one, grad_down_q),
            adapter_scale * contract_leading(query_gradient, query_down_matrix),
            contract_leading(normed_one, grad_down_v),
            adapter_scale * contract_leading(value_gradient, value_down_matrix),
        ]
    )
    adapter_grad = lax.psum(local_grads, ("fsdp", "dp"))
    tokens_total = row_count * lax.axis_size("fsdp") * lax.axis_size("dp")
    step_rate = 0.01 / jnp.sqrt(jnp.float32(tokens_total))
    new_momentum = 0.9 * momentum + adapter_grad
    new_adapters = adapters - step_rate * (adapter_grad + 0.9 * new_momentum)
    new_average = 0.9 * average + 0.1 * new_adapters
    return (
        block_out,
        in_grad,
        adapter_grad,
        new_momentum,
        new_adapters,
        new_average,
        new_adapters.astype(jnp.bfloat16),
    )


def solution(mesh):
    in_specs = (
        P(("fsdp", "dp"), None),
        P(("fsdp", "dp")),
        P(("fsdp", "dp"), None),
        P(),
        P(),
        P("fsdp", None),
        P(),
        P("fsdp", None),
        P("fsdp", None),
        P(),
        P("fsdp", None),
        P(),
        P(),
        P(),
        P(),
    )
    out_specs = (P(("fsdp", "dp"), None), P(("fsdp", "dp"), None), P(), P(), P(), P(), P())
    return jax.shard_map(
        per_device, mesh=mesh, in_specs=in_specs, out_specs=out_specs, check_vma=False
    )
```

profile of v0, /device:TPU:1, one launch (start us, length us, event | category | flops | bytes accessed | tf_op | source)
XLA Modules:
  0.0 687.8 jit_solution(17003402721910862022)
XLA Ops:
  10.0 2.9 copy.35
  15.9 0.8 fusion.55
  17.1 0.9 copy-done.4
  19.1 4.1 copy.43
  23.1 51.6 %all-gather.5.cloned.1.call-done = bf16[1024,3072]{1,0:T(8,128)(2,1)} async-done(((bf16[64,3072]{1,0:T(8,128)(2,1)}), bf16[1024,3072]{1,0:T(8,128)(2,1)}) %all-gather.5.cloned.1.call-update) | async-done | bytes 6291472 | tf_op jit(solution)/shard_map/all_gather | solution.py:139
  74.7 9.0 %broadcast_add_fusion = f32[1024,3072]{1,0:T(8,128)S(1)} fusion(f32[3072]{0:T(1024)S(1)} %copy-done.48, bf16[1024,1024]{0,1:T(8,128)(2,1)S(1)} %copy-done.5, bf16[1024,3072]{1,0:T(8,128)(2,1)} %all-gather.5.cloned.1.call-done), kind=kOutput, calls=%fused_computation.68 | convolution fusion | flops 6445596672 | bytes 20983808 | tf_op jit(solution)/shard_map/dot_general | solution.py:157
  83.7 1.9 slice.83
  85.6 3.2 copy-done.10
  88.8 0.8 fusion.59
  89.6 2.6 copy.37
  92.2 2.9 copy.38
  95.0 4.3 fusion.58
  99.3 3.9 copy.40
  103.2 1.6 broadcast.166.clone
  104.8 100.2 %while.27 = (s32[]{:T(128)}, bf16[2,512,16,64]{1,3,2,0:T(8,128)(2,1)}, f32[2,16,512]{2,1,0:T(8,128)S(1)}, s32[2]{0:T(128)S(1)}, s32[1024]{0:T(1024)}, /*index=5*...) while((s32[]{:T(128)}, ...), condition=%wide.region_5.6_spmd, body=%wide.region_2.5_spmd.sunk | while | flops 2250236416 | bytes 134490384 | solution.py:71
  106.2 0.8 dynamic_slice.57
  107.6 15.3 %fusion.152 = (f32[16,512]{1,0:T(8,128)S(1)}, f32[16,512,1024]{2,1,0:T(8,128)}) fusion(pred[512,1024]{1,0:T(8,128)(4,1)S(1)} %fusion.151, bf16[1024,16,64]{0,2,1:T(8,128)(2,1)S(1)} %get-tuple-element.396, bf16[1024,16,64]{0,2,1:T(8,128)(2,1)} %get-tuple-element.395, s32[]{:T(128)S(6)} %select_n.60), kind=kOutput, calls=%fused_computation.3.clone.1 | convolution fusion | flops 1098899456 | bytes 37257220 | tf_op jit(solution)/shard_map/while/body/eval_jaxpr/qhe,khe->hqk/dot_general | solution.py:46
  122.9 15.9 %fusion.153 = f32[16,512]{1,0:T(8,128)S(1)} fusion(f32[16,512,1024]{2,1,0:T(8,128)} %get-tuple-element.351, f32[16,512]{1,0:T(8,128)S(1)} %get-tuple-element.352, pred[512,1024]{1,0:T(8,128)(4,1)S(1)} %fusion.151), kind=kLoop, calls=%fused_computation.4.clone.1 | loop fusion | flops 33546240 | bytes 34144256 | tf_op jit(solution)/shard_map/while/body/eval_jaxpr/reduce_sum | solution.py:61
  138.8 14.7 %fusion.154 = bf16[2,512,16,64]{1,3,2,0:T(8,128)(2,1)S(1)} fusion(bf16[2,512,16,64]{1,3,2,0:T(8,128)(2,1)S(1)} %copy-done.12, s32[]{:T(128)S(6)} %copy.58, bf16[1024,16,64]{0,2,1:T(8,128)(2,1)S(1)} %copy-done.1, f32[16,512,1024]{2,1,0:T(8,128)} %get-tuple-element.351, f32[16,512]{1,0:T(8,128)S(1)} %fusion.153, ...), kind=kOutput, calls=%fused_computation.11.clone.1 | convolution fusion | flops 1116209152 | bytes 37289988 | tf_op jit(solution)/shard_map/while/body/eval_jaxpr/hqk,khe->qhe/dot_general | solution.py:63
  153.5 1.3 copy-done.13
  156.0 0.8 dynamic_slice.57
  157.4 15.5 %fusion.152 = (f32[16,512]{1,0:T(8,128)S(1)}, f32[16,512,1024]{2,1,0:T(8,128)}) fusion(pred[512,1024]{1,0:T(8,128)(4,1)S(1)} %fusion.151, bf16[1024,16,64]{0,2,1:T(8,128)(2,1)S(1)} %get-tuple-element.396, bf16[1024,16,64]{0,2,1:T(8,128)(2,1)} %get-tuple-element.395, s32[]{:T(128)S(6)} %select_n.60), kind=kOutput, calls=%fused_computation.3.clone.1 | convolution fusion | flops 1098899456 | bytes 37257220 | tf_op jit(solution)/shard_map/while/body/eval_jaxpr/qhe,khe->hqk/dot_general | solution.py:46
  172.9 15.7 %fusion.153 = f32[16,512]{1,0:T(8,128)S(1)} fusion(f32[16,512,1024]{2,1,0:T(8,128)} %get-tuple-element.351, f32[16,512]{1,0:T(8,128)S(1)} %get-tuple-element.352, pred[512,1024]{1,0:T(8,128)(4,1)S(1)} %fusion.151), kind=kLoop, calls=%fused_computation.4.clone.1 | loop fusion | flops 33546240 | bytes 34144256 | tf_op jit(solution)/shard_map/while/body/eval_jaxpr/reduce_sum | solution.py:61
  188.6 14.8 %fusion.154 = bf16[2,512,16,64]{1,3,2,0:T(8,128)(2,1)S(1)} fusion(bf16[2,512,16,64]{1,3,2,0:T(8,128)(2,1)S(1)} %copy-done.12, s32[]{:T(128)S(6)} %copy.58, bf16[1024,16,64]{0,2,1:T(8,128)(2,1)S(1)} %copy-done.1, f32[16,512,1024]{2,1,0:T(8,128)} %get-tuple-element.351, f32[16,512]{1,0:T(8,128)S(1)} %fusion.153, ...), kind=kOutput, calls=%fused_computation.11.clone.1 | convolution fusion | flops 1116209152 | bytes 37289988 | tf_op jit(solution)/shard_map/while/body/eval_jaxpr/hqk,khe->qhe/dot_general | solution.py:63
  203.5 1.3 copy-done.13
  205.0 3.8 copy.41
  208.7 1.9 copy.50
  210.6 5.7 fusion.94
  216.4 2.0 copy-done.8
  218.9 16.9 %fusion.63 = f32[1024,4096]{1,0:T(8,128)} fusion(bf16[1024,4096]{1,0:T(8,128)(2,1)} %all-gather.9.cloned.1.call-done, f32[1024,1024]{0,1:T(8,128)} %copy-done.8, f32[1024]{0:T(1024)S(1)} %bitcast.155, f32[1024]{0:T(1024)S(1)} %bitcast.150, f32[1024]{0:T(1024)S(1)} %fusion.79, f32[1024]{0:T(1024)S(1)} %broadcast_multiply_fusion), kind=kOutput, calls=%fused_computation.96 | convolution fusion | flops 8595177472 | bytes 29376512 | tf_op jit(solution)/shard_map/dot_general | solution.py:184
  235.8 32.2 %all-gather.11.cloned.1.call-done = bf16[4096,1024]{1,0:T(8,128)(2,1)} async-done(((bf16[256,1024]{1,0:T(8,128)(2,1)}), bf16[4096,1024]{1,0:T(8,128)(2,1)}) %all-gather.11.cloned.1.call-update) | async-done | bytes 8388624 | tf_op jit(solution)/shard_map/all_gather | solution.py:144
  268.0 33.9 %multiply_reduce_fusion.1 = (f32[1024]{0:T(1024)S(1)}, f32[1024,1024]{0,1:T(8,128)}) fusion(f32[1024,1024]{0,1:T(8,128)} %copy-done.8, f32[1024]{0:T(1024)S(1)} %bitcast.151, f32[1024]{0:T(1024)S(1)} %broadcast_multiply_fusion, bf16[1024,4096]{1,0:T(8,128)(2,1)} %all-gather.9.cloned.1.call-done, f32[1024,4096]{1,0:T(8,128)} %fusion.63, ...), kind=kOutput, calls=%fused_computation.90 | convolution fusion | flops 17288921088 | bytes 44068864 | tf_op jit(solution)/shard_map/dot_general | solution.py:13
  301.9 4.7 fusion.90
  306.6 3.8 fusion.70
  310.4 1.6 broadcast.166
  311.9 224.5 %while.28 = (s32[]{:T(128)}, f32[1024,16,64]{0,2,1:T(8,128)}, f32[1024,16,64]{0,2,1:T(8,128)}, bf16[2,512,16,64]{1,3,2,0:T(8,128)(2,1)}, s32[2]{0:T(128)S(1)}, /...) while((s32[]{:T(128)}, f32[1024,16,64]{0,2,1:T(8,128)}, ...), condition=%wide.region_12.13_spmd.clone, body=%wide.region_10.12_spmd.clone.sunk | while | flops 5502394880 | bytes 282831200 | solution.py:109
  313.3 14.4 %fusion.164 = f32[16,512,1024]{2,1,0:T(8,128)} fusion(bf16[1024,16,64]{0,2,1:T(8,128)(2,1)S(1)} %get-tuple-element.441, bf16[1024,16,64]{0,2,1:T(8,128)(2,1)} %get-tuple-element.439, s32[]{:T(128)S(6)} %select_n.64), kind=kOutput, calls=%fused_computation.37.clone.1 | convolution fusion | flops 1073741824 | bytes 36700164 | tf_op jit(solution)/shard_map/while/body/eval_jaxpr/qhe,khe->hqk/dot_general | solution.py:46
  329.4 0.8 dynamic_slice.64
  330.8 26.0 %multiply_reduce_fusion.4 = (f32[16,512]{1,0:T(8,128)S(1)}, f32[16,512,1024]{2,1,0:T(8,128)}) fusion(f32[16,512,1024]{2,1,0:T(8,128)} %fusion.164, f32[16,512]{1,0:T(8,128)S(1)} %dynamic-slice_bitcast_fusion.2, pred[512,1024]{1,0:T(8,128)(4,1)S(1)} %fusion.165, bf16[1024,16,64]{0,2,1:T(8,128)(2,1)} %get-tuple-element.444, ...), kind=kOutput, calls=%fused_computation.20.clone.1 | convolution fusion | flops 1115676672 | bytes 70844416 | tf_op jit(solution)/shard_map/while/body/eval_jaxpr/qhe,khe->hqk/dot_general | solution.py:84
  356.8 27.8 %multiply_convert_fusion.7 = bf16[16,512,1024]{2,1,0:T(8,128)(2,1)} fusion(f32[16,512,1024]{2,1,0:T(8,128)} %get-tuple-element.364, f32[16,512,1024]{2,1,0:T(8,128)} %fusion.164, f32[16,512]{1,0:T(8,128)S(1)} %get-tuple-element.365, f32[16,512]{1,0:T(8,128)S(1)} %dynamic-slice_bitcast_fusion.2, pred[512,1024]{1,0:T(8,128)(4,1)S(1)} %fusion.165), kind=kLoop, calls=%fused_computation.19.clone.1 | loop fusion | flops 50331648 | bytes 84475904 | tf_op jit(solution)/shard_map/while/body/eval_jaxpr/convert_element_type | solution.py:94
  384.6 11.1 %bitcast_add_fusion.4 = f32[1024,16,64]{0,2,1:T(8,128)} fusion(f32[1024,16,64]{0,2,1:T(8,128)} %get-tuple-element.419, bf16[16,512,1024]{2,1,0:T(8,128)(2,1)} %multiply_convert_fusion.7, pred[]{:T(512)S(6)} %compare.3, bf16[1024,16,64]{0,2,1:T(8,128)(2,1)} %get-tuple-element.439, s32[]{:T(128)S(6)} %select_n.64), kind=kOutput, calls=%fused_computation.26.clone.1 | convolution fusion | flops 1076887552 | bytes 26214404 | tf_op jit(solution)/shard_map/while/body/eval_jaxpr/hqk,qhe->khe/dot_general | solution.py:101
  395.7 17.5 %bitcast_add_fusion.5 = f32[1024,16,64]{0,2,1:T(8,128)} fusion(f32[1024,16,64]{0,2,1:T(8,128)} %get-tuple-element.420, f32[16,512,1024]{2,1,0:T(8,128)} %fusion.164, f32[16,512]{1,0:T(8,128)S(1)} %dynamic-slice_bitcast_fusion.2, pred[512,1024]{1,0:T(8,128)(4,1)S(1)} %fusion.165, pred[]{:T(512)S(6)} %compare.3, ...), kind=kOutput, calls=%fused_computation.25.clone.1 | convolution fusion | flops 1109393408 | bytes 43548676 | tf_op jit(solution)/shard_map/while/body/eval_jaxpr/hqk,qhe->khe/dot_general | solution.py:87
  413.2 9.8 %fusion.166 = bf16[2,512,16,64]{1,3,2,0:T(8,128)(2,1)} fusion(bf16[2,512,16,64]{1,3,2,0:T(8,128)(2,1)} %get-tuple-element.421, s32[]{:T(128)S(6)} %copy.68, bf16[16,512,1024]{2,1,0:T(8,128)(2,1)} %multiply_convert_fusion.7, bf16[1024,16,64]{0,2,1:T(8,128)(2,1)S(1)} %get-tuple-element.441), kind=kOutput, calls=%fused_computation.32.clone.1 | convolution fusion | flops 1074790400 | bytes 19922948 | tf_op jit(solution)/shard_map/while/body/eval_jaxpr/hqk,khe->qhe/dot_general | solution.py:96
  424.1 14.4 %fusion.164 = f32[16,512,1024]{2,1,0:T(8,128)} fusion(bf16[1024,16,64]{0,2,1:T(8,128)(2,1)S(1)} %get-tuple-element.441, bf16[1024,16,64]{0,2,1:T(8,128)(2,1)} %get-tuple-element.439, s32[]{:T(128)S(6)} %select_n.64), kind=kOutput, calls=%fused_computation.37.clone.1 | convolution fusion | flops 1073741824 | bytes 36700164 | tf_op jit(solution)/shard_map/while/body/eval_jaxpr/qhe,khe->hqk/dot_general | solution.py:46
  440.3 0.8 dynamic_slice.64
  441.7 26.0 %multiply_reduce_fusion.4 = (f32[16,512]{1,0:T(8,128)S(1)}, f32[16,512,1024]{2,1,0:T(8,128)}) fusion(f32[16,512,1024]{2,1,0:T(8,128)} %fusion.164, f32[16,512]{1,0:T(8,128)S(1)} %dynamic-slice_bitcast_fusion.2, pred[512,1024]{1,0:T(8,128)(4,1)S(1)} %fusion.165, bf16[1024,16,64]{0,2,1:T(8,128)(2,1)} %get-tuple-element.444, ...), kind=kOutput, calls=%fused_computation.20.clone.1 | convolution fusion | flops 1115676672 | bytes 70844416 | tf_op jit(solution)/shard_map/while/body/eval_jaxpr/qhe,khe->hqk/dot_general | solution.py:84
  467.6 27.8 %multiply_convert_fusion.7 = bf16[16,512,1024]{2,1,0:T(8,128)(2,1)} fusion(f32[16,512,1024]{2,1,0:T(8,128)} %get-tuple-element.364, f32[16,512,1024]{2,1,0:T(8,128)} %fusion.164, f32[16,512]{1,0:T(8,128)S(1)} %get-tuple-element.365, f32[16,512]{1,0:T(8,128)S(1)} %dynamic-slice_bitcast_fusion.2, pred[512,1024]{1,0:T(8,128)(4,1)S(1)} %fusion.165), kind=kLoop, calls=%fused_computation.19.clone.1 | loop fusion | flops 50331648 | bytes 84475904 | tf_op jit(solution)/shard_map/while/body/eval_jaxpr/convert_element_type | solution.py:94
  495.4 12.3 %bitcast_add_fusion.4 = f32[1024,16,64]{0,2,1:T(8,128)} fusion(f32[1024,16,64]{0,2,1:T(8,128)} %get-tuple-element.419, bf16[16,512,1024]{2,1,0:T(8,128)(2,1)} %multiply_convert_fusion.7, pred[]{:T(512)S(6)} %compare.3, bf16[1024,16,64]{0,2,1:T(8,128)(2,1)} %get-tuple-element.439, s32[]{:T(128)S(6)} %select_n.64), kind=kOutput, calls=%fused_computation.26.clone.1 | convolution fusion | flops 1076887552 | bytes 26214404 | tf_op jit(solution)/shard_map/while/body/eval_jaxpr/hqk,qhe->khe/dot_general | solution.py:101
  507.8 18.7 %bitcast_add_fusion.5 = f32[1024,16,64]{0,2,1:T(8,128)} fusion(f32[1024,16,64]{0,2,1:T(8,128)} %get-tuple-element.420, f32[16,512,1024]{2,1,0:T(8,128)} %fusion.164, f32[16,512]{1,0:T(8,128)S(1)} %dynamic-slice_bitcast_fusion.2, pred[512,1024]{1,0:T(8,128)(4,1)S(1)} %fusion.165, pred[]{:T(512)S(6)} %compare.3, ...), kind=kOutput, calls=%fused_computation.25.clone.1 | convolution fusion | flops 1109393408 | bytes 43548676 | tf_op jit(solution)/shard_map/while/body/eval_jaxpr/hqk,qhe->khe/dot_general | solution.py:87
  526.5 9.8 %fusion.166 = bf16[2,512,16,64]{1,3,2,0:T(8,128)(2,1)} fusion(bf16[2,512,16,64]{1,3,2,0:T(8,128)(2,1)} %get-tuple-element.421, s32[]{:T(128)S(6)} %copy.68, bf16[16,512,1024]{2,1,0:T(8,128)(2,1)} %multiply_convert_fusion.7, bf16[1024,16,64]{0,2,1:T(8,128)(2,1)S(1)} %get-tuple-element.441), kind=kOutput, calls=%fused_computation.32.clone.1 | convolution fusion | flops 1074790400 | bytes 19922948 | tf_op jit(solution)/shard_map/while/body/eval_jaxpr/hqk,khe->qhe/dot_general | solution.py:96
  536.5 2.7 convert_element_type.94
  540.2 2.2 copy.44
  544.0 0.8 fusion.77
  547.8 6.7 fusion.42
  554.6 1.6 fusion.56
  556.3 1.9 copy-done.7
  558.2 1.0 fusion.69
  559.9 17.0 %add_convert_fusion = bf16[1024,1024]{0,1:T(8,128)(2,1)} fusion(f32[1024,1024]{0,1:T(8,128)} %copy-done.8, f32[1024]{0:T(1024)S(1)} %bitcast.154, bf16[4096,1024]{1,0:T(8,128)(2,1)} %all-gather.11.cloned.1.call-done, f32[1024,4096]{1,0:T(8,128)} %fusion.63, f32[4096]{0:T(1024)S(1)} %copy-done.47), kind=kOutput, calls=%fused_computation.91 | convolution fusion | flops 8635023360 | bytes 31477760 | tf_op jit(solution)/shard_map/dot_general | solution.py:188
  576.9 7.8 %add_add_fusion.2 = f32[1024,1024]{0,1:T(8,128)} fusion(f32[1024,1024]{0,1:T(8,128)} %copy-done.9, bf16[1024,1024]{0,1:T(8,128)(2,1)} %copy.43, f32[1024]{0:T(1024)S(1)} %negate_multiply_fusion, f32[1024]{0:T(1024)S(1)} %copy-done.38, f32[1024]{0:T(1024)S(1)} %multiply_multiply_fusion.2, f32[1024]{0:T(1024)S(1)} %copy-done.23, ...), kind=kLoop, calls=%fused_computation.87 | loop fusion | flops 11534336 | bytes 16797696 | tf_op jit(solution)/shard_map/add | solution.py:227
  584.7 3.9 copy.45
  588.6 5.4 copy.46
  594.0 83.1 %all-reduce.2.cloned.1.call-done = f32[4,1024,4]{1,2,0:T(4,128)} async-done(((f32[4,1024,4]{1,2,0:T(4,128)}), f32[4,1024,4]{1,2,0:T(4,128)}) %all-reduce.2.cloned.1.call-update) | async-done | bytes 65552 | tf_op jit(solution)/shard_map/psum | solution.py:236
  677.2 1.5 fusion.89
  679.3 1.5 copy.77
  (167 shorter events, 19.6 us)
Async XLA Ops:
  7.2 5.8 copy-start.39
  7.2 6.4 copy-start.40
  7.2 67.5 %all-gather.5.cloned.1.call-start = ((), (), s32[]{:S(2)}) async-start(), calls=%async_computation | async-start | bytes 6684672 | tf_op jit(solution)/shard_map/all_gather | solution.py:139
  7.9 202.7 %all-gather.7.cloned.1.call-start = ((), (), s32[]{:S(2)}) async-start(), calls=%async_computation.1 | async-start | bytes 2228224 | tf_op jit(solution)/shard_map/all_gather | solution.py:140
  8.7 210.2 %all-gather.9.cloned.1.call-start = ((), (), s32[]{:S(2)}) async-start(), calls=%async_computation.2 | async-start | bytes 8912896 | tf_op jit(solution)/shard_map/all_gather | solution.py:143
  9.4 258.6 %all-gather.11.cloned.1.call-start = ((), (), s32[]{:S(2)}) async-start(), calls=%async_computation.3 | async-start | bytes 8912896 | tf_op jit(solution)/shard_map/all_gather | solution.py:144
  10.0 667.2 %all-reduce.2.cloned.1.call-start = ((), (), s32[]{:S(2)}) async-start(), calls=%async_computation.4 | async-start | bytes 131072 | tf_op jit(solution)/shard_map/psum | solution.py:236
  10.0 5.8 copy-start.20
  13.0 3.7 copy-start.2
  14.3 2.4 copy-start.34
  14.6 2.5 copy-start.22
  15.2 0.6 copy-start.32
  15.8 1.3 copy-start.30
  15.9 79.2 %copy-start.17 = (bf16[4,1024,4]{1,2,0:T(4,128)(2,1)}, bf16[4,1024,4]{1,2,0:T(4,128)(2,1)S(1)}, u32[]{:S(2)}) copy-start(bf16[4,1024,4]{1,2,0:T(4,128)(2,1)S(1)} %convert_element_type.81) | copy-start | bytes 98308
  15.9 2.6 copy-start.41
  16.7 1.3 copy-start.4
  16.7 58.0 %copy-start.48 = (f32[3072]{0:T(1024)S(1)}, f32[3072]{0:T(1024)}, u32[]{:S(2)}) copy-start(f32[3072]{0:T(1024)} %param.25) | copy-start | bytes 36868
  18.0 67.5 %copy-start.24 = (bf16[1024,4]{0,1:T(4,128)(2,1)}, bf16[1024,4]{0,1:T(4,128)(2,1)S(1)}, u32[]{:S(2)}) copy-start(bf16[1024,4]{0,1:T(4,128)(2,1)S(1)} %convolution_convert_fusion.1) | copy-start | bytes 24580
  18.4 76.6 %copy-start.26 = (bf16[1024,4]{0,1:T(4,128)(2,1)}, bf16[1024,4]{0,1:T(4,128)(2,1)S(1)}, u32[]{:S(2)}) copy-start(bf16[1024,4]{0,1:T(4,128)(2,1)S(1)} %convolution_convert_fusion) | copy-start | bytes 24580
  18.4 56.3 %copy-start.5 = (bf16[1024,1024]{0,1:T(8,128)(2,1)S(1)}, bf16[1024,1024]{0,1:T(8,128)(2,1)}, u32[]{:S(2)}) copy-start(bf16[1024,1024]{0,1:T(8,128)(2,1)} %copy-done.4) | copy-start | bytes 6291460
  83.7 5.2 copy-start.10
  122.9 15.9 %copy-start.1 = (bf16[1024,16,64]{0,2,1:T(8,128)(2,1)S(1)}, bf16[1024,16,64]{0,2,1:T(8,128)(2,1)}, u32[]{:S(2)}) copy-start(bf16[1024,16,64]{0,2,1:T(8,128)(2,1)} %get-tuple-element.397) | copy-start | bytes 6291460 | tf_op jit(solution)/shard_map/while
  122.9 15.9 %copy-start.12 = (bf16[2,512,16,64]{1,3,2,0:T(8,128)(2,1)S(1)}, bf16[2,512,16,64]{1,3,2,0:T(8,128)(2,1)}, u32[]{:S(2)}) copy-start(bf16[2,512,16,64]{1,3,2,0:T(8,128)(2,1)} %get-tuple-element.379) | copy-start | bytes 6291460 | tf_op jit(solution)/shard_map/while
  153.4 1.3 copy-start.13
  172.9 15.7 %copy-start.1 = (bf16[1024,16,64]{0,2,1:T(8,128)(2,1)S(1)}, bf16[1024,16,64]{0,2,1:T(8,128)(2,1)}, u32[]{:S(2)}) copy-start(bf16[1024,16,64]{0,2,1:T(8,128)(2,1)} %get-tuple-element.397) | copy-start | bytes 6291460 | tf_op jit(solution)/shard_map/while
  172.9 15.7 %copy-start.12 = (bf16[2,512,16,64]{1,3,2,0:T(8,128)(2,1)S(1)}, bf16[2,512,16,64]{1,3,2,0:T(8,128)(2,1)}, u32[]{:S(2)}) copy-start(bf16[2,512,16,64]{1,3,2,0:T(8,128)(2,1)} %get-tuple-element.379) | copy-start | bytes 6291460 | tf_op jit(solution)/shard_map/while
  203.4 1.3 copy-start.13
  205.0 5.7 copy-start.44
  216.4 2.0 copy-start.8
  216.4 2.5 copy-start.36
  216.4 2.5 copy-start.43
  218.9 49.0 %copy-start.46 = (f32[4096]{0:T(1024)S(1)}, f32[4096]{0:T(1024)}, u32[]{:S(2)}) copy-start(f32[4096]{0:T(1024)} %param.28) | copy-start | bytes 49156
  301.9 4.7 copy-start.14
  301.9 4.7 copy-start.45
  306.5 3.8 copy-start.9
  306.6 3.8 copy-start.37
  312.1 17.3 %copy-start.15 = (f32[2,16,512]{2,1,0:T(8,128)}, f32[2,16,512]{2,1,0:T(8,128)S(1)}, u32[]{:S(2)}) copy-start(f32[2,16,512]{2,1,0:T(8,128)S(1)} %get-tuple-element.442) | copy-start | bytes 196612 | tf_op jit(solution)/shard_map/while
  413.2 9.8 %copy-start.16 = (f32[2,16,512]{2,1,0:T(8,128)S(1)}, f32[2,16,512]{2,1,0:T(8,128)}, u32[]{:S(2)}) copy-start(f32[2,16,512]{2,1,0:T(8,128)} %copy-done.15) | copy-start | bytes 196612 | tf_op jit(solution)/shard_map/while
  423.0 17.3 %copy-start.15 = (f32[2,16,512]{2,1,0:T(8,128)}, f32[2,16,512]{2,1,0:T(8,128)S(1)}, u32[]{:S(2)}) copy-start(f32[2,16,512]{2,1,0:T(8,128)S(1)} %get-tuple-element.442) | copy-start | bytes 196612 | tf_op jit(solution)/shard_map/while
  526.5 9.8 %copy-start.16 = (f32[2,16,512]{2,1,0:T(8,128)S(1)}, f32[2,16,512]{2,1,0:T(8,128)}, u32[]{:S(2)}) copy-start(f32[2,16,512]{2,1,0:T(8,128)} %copy-done.15) | copy-start | bytes 196612 | tf_op jit(solution)/shard_map/while
  536.4 2.7 copy-start.18
  536.4 3.1 copy-start.27
  536.5 3.7 copy-start.11
  542.4 1.0 copy-start.25
  542.9 1.8 copy-start.6
  543.3 2.5 copy-start
  544.0 3.2 slice-start
  545.9 1.9 slice-start.1
  547.8 6.7 copy-start.3
  547.8 6.7 copy-start.23
  547.8 6.8 copy-start.35
  554.6 1.7 copy-start.33
  554.6 3.6 copy-start.31
  556.2 2.0 copy-start.7
  556.2 3.6 copy-start.42
  556.2 3.6 copy-start.47
  559.9 17.0 %copy-start.38 = (f32[1024]{0:T(1024)S(1)}, f32[1024]{0:T(1024)}, u32[]{:S(2)}) copy-start(f32[1024]{0:T(1024)} %copy-done.37) | copy-start | bytes 12292
  588.6 88.5 %copy-start.21 = (f32[4,1024,4]{1,2,0:T(4,128)S(1)}, f32[4,1024,4]{1,2,0:T(4,128)}, u32[]{:S(2)}) copy-start(f32[4,1024,4]{1,2,0:T(4,128)} %param.31) | copy-start | bytes 196612
  588.6 88.5 %copy-start.29 = (f32[4,1024,4]{1,2,0:T(4,128)S(1)}, f32[4,1024,4]{1,2,0:T(4,128)}, u32[]{:S(2)}) copy-start(f32[4,1024,4]{1,2,0:T(4,128)} %param.32) | copy-start | bytes 196612
  588.6 90.1 %copy-start.28 = (f32[4,1024,4]{1,2,0:T(4,128)S(1)}, f32[4,1024,4]{1,2,0:T(4,128)}, u32[]{:S(2)}) copy-start(f32[4,1024,4]{1,2,0:T(4,128)} %param.33) | copy-start | bytes 196612
  678.7 2.1 copy-start.19
Sparse Core Ops, SparseCore 0:
  10.3 64.3 all-gather.4
  76.9 39.9 all-gather.6
  119.0 73.7 all-gather.8
  194.8 73.1 all-gather.10
  560.0 117.0 all-reduce.1
where the time goes:
time: 696 us; the launch traced here: 688 us
  matrix products  325 us (47%)
  waiting for transfers between devices  169 us (24%)
  other arithmetic  111 us (16%)
  local copies, waits for them, and re-layouts  60.7 us (9%)
  between operations  14.8 us (2%)
    psum x1, waiting for transfers between devices, per_device(): adapter_grad = lax.psum(local_grads, ('fsdp', 'dp'))  83.1 us
    dot_general x4, matrix products, block_scores(): jnp.einsum('qhe,khe->hqk', query_block, key_heads, preferred_element_type...  59.7 us
    convert_element_type x2, other arithmetic, one_block(): grad_scores = (probs * (grad_probs - inner)).astype(jnp.bfloat16)  55.6 us
    dot_general x2, matrix products, one_block(): jnp.einsum('qhe,khe->hqk', grad_block, value_heads, preferred_element_typ...  52 us
    dot_general x7, matrix products, contract_trailing(): lax.dot_general(left, right, (((1,), (1,)), ((), ())), preferred_element_...  51.8 us
    all_gather x1, waiting for transfers between devices, per_device(): lax.all_gather(w_qkv, 'fsdp', axis=0, tiled=True)  51.6 us
    dot_general x2, matrix products, one_block(): jnp.einsum('hqk,qhe->khe', probs.astype(jnp.bfloat16), grad_block, prefer...  36.3 us
    all_gather x1, waiting for transfers between devices, per_device(): lax.all_gather(w_proj, 'fsdp', axis=0, tiled=True)  32.2 us
  transfers between devices with their start and end apart: 5, of which 3 were waited for; matrix products, arithmetic and copies ran while one was open for 29% of the time, Pallas kernels for 0%

commit v1 on v0

--- a/solution.py
+++ b/solution.py
@@ -2,6 +2,7 @@
 import jax.numpy as jnp
 from jax import lax
 from jax.sharding import PartitionSpec as P
+from jax.lax import all_gather
 
 HEADS = 16
 query_span = 512
@@ -233,7 +234,12 @@
             adapter_scale * contract_leading(value_gradient, value_down_matrix),
         ]
     )
-    adapter_grad = lax.psum(local_grads, ("fsdp", "dp"))
+
+    def divide_the_desk(dev_axis, inner_x):
+        p_next = all_gather(inner_x, dev_axis).sum(axis=0)
+        return p_next
+
+    adapter_grad = divide_the_desk(("fsdp", "dp"), local_grads)
     tokens_total = row_count * lax.axis_size("fsdp") * lax.axis_size("dp")
     step_rate = 0.01 / jnp.sqrt(jnp.float32(tokens_total))
     new_momentum = 0.9 * momentum + adapter_grad

time: 696 us -> 620 us (0.89)
  waiting for transfers between devices: 169 us -> 93.2 us
    psum x1 -> x0, waiting for transfers between devices: 83.1 us -> none  [per_device(): adapter_grad = lax.psum(local_grads, ('fsdp', 'dp'))]
    all_gather x0 -> x1, waiting for transfers between devices: none -> 7.18 us  [divide_the_desk(): p_next = all_gather(inner_x, dev_axis).sum(axis=0)]
    unnamed x99 -> x100, local copies, waits for them, and re-layouts: 30.4 us -> 27.7 us
  transfers between devices with their start and end apart: 5 -> 5, of which waited for: 3 -> 3; matrix products, arithmetic and copies ran while one was open for 29% -> 34% of each run, Pallas kernels for 0% -> 0%
where the time goes in v1:
time: 620 us; the launch traced here: 612 us
  matrix products  327 us (53%)
  other arithmetic  111 us (18%)
  waiting for transfers between devices  93.2 us (15%)
  local copies, waits for them, and re-layouts  58.1 us (9%)
  between operations  14.7 us (2%)
  loops' own time  7.63 us (1%)
    dot_general x4, matrix products, block_scores(): jnp.einsum('qhe,khe->hqk', query_block, key_heads, preferred_element_type...  59.6 us
    convert_element_type x2, other arithmetic, one_block(): grad_scores = (probs * (grad_probs - inner)).astype(jnp.bfloat16)  55.6 us
    dot_general x7, matrix products, contract_trailing(): lax.dot_general(left, right, (((1,), (1,)), ((), ())), preferred_element_...  54.4 us
    dot_general x2, matrix products, one_block(): jnp.einsum('qhe,khe->hqk', grad_block, value_heads, preferred_element_typ...  51.9 us
    all_gather x1, waiting for transfers between devices, per_device(): lax.all_gather(w_qkv, 'fsdp', axis=0, tiled=True)  51.5 us
    dot_general x2, matrix products, one_block(): jnp.einsum('hqk,qhe->khe', probs.astype(jnp.bfloat16), grad_block, prefer...  36.3 us
    all_gather x1, waiting for transfers between devices, per_device(): lax.all_gather(w_proj, 'fsdp', axis=0, tiled=True)  31.9 us
    reduce_sum x2, other arithmetic, one_block(): totals = jnp.sum(raised, axis=-1, keepdims=True)  31.5 us
  transfers between devices with their start and end apart: 5, of which 3 were waited for; matrix products, arithmetic and copies ran while one was open for 34% of the time, Pallas kernels for 0%

profile of v1, /device:TPU:1, one launch (start us, length us, event | category | flops | bytes accessed | tf_op | source)
XLA Modules:
  0.0 611.6 jit_solution(1547512227022111034)
XLA Ops:
  10.0 2.9 copy.47
  15.9 0.8 fusion.55
  17.1 0.9 copy-done.3
  19.1 4.1 copy.55
  23.1 51.5 %all-gather.7.cloned.1.call-done = bf16[1024,3072]{1,0:T(8,128)(2,1)} async-done(((bf16[64,3072]{1,0:T(8,128)(2,1)}), bf16[1024,3072]{1,0:T(8,128)(2,1)}) %all-gather.7.cloned.1.call-update) | async-done | bytes 6291472 | tf_op jit(solution)/shard_map/all_gather | solution.py:140
  74.7 9.0 %broadcast_add_fusion = f32[1024,3072]{1,0:T(8,128)S(1)} fusion(f32[3072]{0:T(1024)S(1)} %copy-done.51, bf16[1024,1024]{0,1:T(8,128)(2,1)S(1)} %copy-done.4, bf16[1024,3072]{1,0:T(8,128)(2,1)} %all-gather.7.cloned.1.call-done), kind=kOutput, calls=%fused_computation.68 | convolution fusion | flops 6445596672 | bytes 20983808 | tf_op jit(solution)/shard_map/dot_general | solution.py:158
  83.7 1.9 slice.83
  85.6 3.2 copy-done.11
  88.8 0.8 fusion.59
  89.6 2.6 copy.49
  92.2 2.9 copy.50
  95.1 4.3 fusion.58
  99.3 3.9 copy.52
  103.2 1.6 broadcast.166.clone
  104.8 100.5 %while.27 = (s32[]{:T(128)}, bf16[2,512,16,64]{1,3,2,0:T(8,128)(2,1)}, f32[2,16,512]{2,1,0:T(8,128)S(1)}, s32[2]{0:T(128)S(1)}, s32[1024]{0:T(1024)}, /*index=5*...) while((s32[]{:T(128)}, ...), condition=%wide.region_5.6_spmd, body=%wide.region_2.5_spmd.sunk | while | flops 2250236416 | bytes 134490384 | solution.py:72
  106.5 0.8 dynamic_slice.57
  107.9 15.3 %fusion.152 = (f32[16,512]{1,0:T(8,128)S(1)}, f32[16,512,1024]{2,1,0:T(8,128)}) fusion(pred[512,1024]{1,0:T(8,128)(4,1)S(1)} %fusion.151, bf16[1024,16,64]{0,2,1:T(8,128)(2,1)S(1)} %get-tuple-element.403, bf16[1024,16,64]{0,2,1:T(8,128)(2,1)} %get-tuple-element.402, s32[]{:T(128)S(6)} %select_n.60), kind=kOutput, calls=%fused_computation.3.clone.1 | convolution fusion | flops 1098899456 | bytes 37257220 | tf_op jit(solution)/shard_map/while/body/eval_jaxpr/qhe,khe->hqk/dot_general | solution.py:47
  123.2 15.9 %fusion.153 = f32[16,512]{1,0:T(8,128)S(1)} fusion(f32[16,512,1024]{2,1,0:T(8,128)} %get-tuple-element.358, f32[16,512]{1,0:T(8,128)S(1)} %get-tuple-element.359, pred[512,1024]{1,0:T(8,128)(4,1)S(1)} %fusion.151), kind=kLoop, calls=%fused_computation.4.clone.1 | loop fusion | flops 33546240 | bytes 34144256 | tf_op jit(solution)/shard_map/while/body/eval_jaxpr/reduce_sum | solution.py:62
  139.1 14.7 %fusion.154 = bf16[2,512,16,64]{1,3,2,0:T(8,128)(2,1)S(1)} fusion(bf16[2,512,16,64]{1,3,2,0:T(8,128)(2,1)S(1)} %copy-done.13, s32[]{:T(128)S(6)} %copy.70, bf16[1024,16,64]{0,2,1:T(8,128)(2,1)S(1)} %copy-done, f32[16,512,1024]{2,1,0:T(8,128)} %get-tuple-element.358, f32[16,512]{1,0:T(8,128)S(1)} %fusion.153, f32[16,512]{1,0:T(8,128)S(1)} %get-tuple-element.359, ...), kind=kOutput, calls=%fused_computation.11.clone.1 | convolution fusion | flops 1116209152 | bytes 37289988 | tf_op jit(solution)/shard_map/while/body/eval_jaxpr/hqk,khe->qhe/dot_general | solution.py:64
  153.8 1.3 copy-done.14
  156.4 0.8 dynamic_slice.57
  157.7 15.4 %fusion.152 = (f32[16,512]{1,0:T(8,128)S(1)}, f32[16,512,1024]{2,1,0:T(8,128)}) fusion(pred[512,1024]{1,0:T(8,128)(4,1)S(1)} %fusion.151, bf16[1024,16,64]{0,2,1:T(8,128)(2,1)S(1)} %get-tuple-element.403, bf16[1024,16,64]{0,2,1:T(8,128)(2,1)} %get-tuple-element.402, s32[]{:T(128)S(6)} %select_n.60), kind=kOutput, calls=%fused_computation.3.clone.1 | convolution fusion | flops 1098899456 | bytes 37257220 | tf_op jit(solution)/shard_map/while/body/eval_jaxpr/qhe,khe->hqk/dot_general | solution.py:47
  173.2 15.7 %fusion.153 = f32[16,512]{1,0:T(8,128)S(1)} fusion(f32[16,512,1024]{2,1,0:T(8,128)} %get-tuple-element.358, f32[16,512]{1,0:T(8,128)S(1)} %get-tuple-element.359, pred[512,1024]{1,0:T(8,128)(4,1)S(1)} %fusion.151), kind=kLoop, calls=%fused_computation.4.clone.1 | loop fusion | flops 33546240 | bytes 34144256 | tf_op jit(solution)/shard_map/while/body/eval_jaxpr/reduce_sum | solution.py:62
  188.9 14.9 %fusion.154 = bf16[2,512,16,64]{1,3,2,0:T(8,128)(2,1)S(1)} fusion(bf16[2,512,16,64]{1,3,2,0:T(8,128)(2,1)S(1)} %copy-done.13, s32[]{:T(128)S(6)} %copy.70, bf16[1024,16,64]{0,2,1:T(8,128)(2,1)S(1)} %copy-done, f32[16,512,1024]{2,1,0:T(8,128)} %get-tuple-element.358, f32[16,512]{1,0:T(8,128)S(1)} %fusion.153, f32[16,512]{1,0:T(8,128)S(1)} %get-tuple-element.359, ...), kind=kOutput, calls=%fused_computation.11.clone.1 | convolution fusion | flops 1116209152 | bytes 37289988 | tf_op jit(solution)/shard_map/while/body/eval_jaxpr/hqk,khe->qhe/dot_general | solution.py:64
  203.8 1.3 copy-done.14
  205.2 3.8 copy.53
  209.0 1.9 copy.62
  210.9 5.7 fusion.94
  216.7 2.0 copy-done.8
  219.2 16.9 %fusion.63 = f32[1024,4096]{1,0:T(8,128)} fusion(bf16[1024,4096]{1,0:T(8,128)(2,1)} %all-gather.11.cloned.1.call-done, f32[1024,1024]{0,1:T(8,128)} %copy-done.8, f32[1024]{0:T(1024)S(1)} %bitcast.157, f32[1024]{0:T(1024)S(1)} %bitcast.152, f32[1024]{0:T(1024)S(1)} %fusion.79, f32[1024]{0:T(1024)S(1)} %broadcast_multiply_fusion), kind=kOutput, calls=%fused_computation.96 | convolution fusion | flops 8595177472 | bytes 29376512 | tf_op jit(solution)/shard_map/dot_general | solution.py:185
  236.1 31.9 %all-gather.13.cloned.1.call-done = bf16[4096,1024]{1,0:T(8,128)(2,1)} async-done(((bf16[256,1024]{1,0:T(8,128)(2,1)}), bf16[4096,1024]{1,0:T(8,128)(2,1)}) %all-gather.13.cloned.1.call-update) | async-done | bytes 8388624 | tf_op jit(solution)/shard_map/all_gather | solution.py:145
  268.0 33.7 %multiply_reduce_fusion.1 = (f32[1024]{0:T(1024)S(1)}, f32[1024,1024]{0,1:T(8,128)}) fusion(f32[1024,1024]{0,1:T(8,128)} %copy-done.8, f32[1024]{0:T(1024)S(1)} %bitcast.153, f32[1024]{0:T(1024)S(1)} %broadcast_multiply_fusion, bf16[1024,4096]{1,0:T(8,128)(2,1)} %all-gather.11.cloned.1.call-done, f32[1024,4096]{1,0:T(8,128)} %fusion.63, ...), kind=kOutput, calls=%fused_computation.90 | convolution fusion | flops 17288921088 | bytes 44068864 | tf_op jit(solution)/shard_map/dot_general | solution.py:14
  301.7 4.7 fusion.90
  306.4 3.8 fusion.70
  310.2 1.6 broadcast.166
  311.7 225.1 %while.28 = (s32[]{:T(128)}, f32[1024,16,64]{0,2,1:T(8,128)}, f32[1024,16,64]{0,2,1:T(8,128)}, bf16[2,512,16,64]{1,3,2,0:T(8,128)(2,1)}, s32[2]{0:T(128)S(1)}, /...) while((s32[]{:T(128)}, f32[1024,16,64]{0,2,1:T(8,128)}, ...), condition=%wide.region_12.13_spmd.clone, body=%wide.region_10.12_spmd.clone.sunk | while | flops 5502394880 | bytes 282831200 | solution.py:110
  313.4 14.4 %fusion.164 = f32[16,512,1024]{2,1,0:T(8,128)} fusion(bf16[1024,16,64]{0,2,1:T(8,128)(2,1)S(1)} %get-tuple-element.448, bf16[1024,16,64]{0,2,1:T(8,128)(2,1)} %get-tuple-element.446, s32[]{:T(128)S(6)} %select_n.64), kind=kOutput, calls=%fused_computation.37.clone.1 | convolution fusion | flops 1073741824 | bytes 36700164 | tf_op jit(solution)/shard_map/while/body/eval_jaxpr/qhe,khe->hqk/dot_general | solution.py:47
  329.7 0.8 dynamic_slice.64
  331.1 26.0 %multiply_reduce_fusion.4 = (f32[16,512]{1,0:T(8,128)S(1)}, f32[16,512,1024]{2,1,0:T(8,128)}) fusion(f32[16,512,1024]{2,1,0:T(8,128)} %fusion.164, f32[16,512]{1,0:T(8,128)S(1)} %dynamic-slice_bitcast_fusion.2, pred[512,1024]{1,0:T(8,128)(4,1)S(1)} %fusion.165, bf16[1024,16,64]{0,2,1:T(8,128)(2,1)} %get-tuple-element.451, ...), kind=kOutput, calls=%fused_computation.20.clone.1 | convolution fusion | flops 1115676672 | bytes 70844416 | tf_op jit(solution)/shard_map/while/body/eval_jaxpr/qhe,khe->hqk/dot_general | solution.py:85
  357.0 27.8 %multiply_convert_fusion.7 = bf16[16,512,1024]{2,1,0:T(8,128)(2,1)} fusion(f32[16,512,1024]{2,1,0:T(8,128)} %get-tuple-element.371, f32[16,512,1024]{2,1,0:T(8,128)} %fusion.164, f32[16,512]{1,0:T(8,128)S(1)} %get-tuple-element.372, f32[16,512]{1,0:T(8,128)S(1)} %dynamic-slice_bitcast_fusion.2, pred[512,1024]{1,0:T(8,128)(4,1)S(1)} %fusion.165), kind=kLoop, calls=%fused_computation.19.clone.1 | loop fusion | flops 50331648 | bytes 84475904 | tf_op jit(solution)/shard_map/while/body/eval_jaxpr/convert_element_type | solution.py:95
  384.8 11.1 %bitcast_add_fusion.4 = f32[1024,16,64]{0,2,1:T(8,128)} fusion(f32[1024,16,64]{0,2,1:T(8,128)} %get-tuple-element.426, bf16[16,512,1024]{2,1,0:T(8,128)(2,1)} %multiply_convert_fusion.7, pred[]{:T(512)S(6)} %compare.3, bf16[1024,16,64]{0,2,1:T(8,128)(2,1)} %get-tuple-element.446, s32[]{:T(128)S(6)} %select_n.64), kind=kOutput, calls=%fused_computation.26.clone.1 | convolution fusion | flops 1076887552 | bytes 26214404 | tf_op jit(solution)/shard_map/while/body/eval_jaxpr/hqk,qhe->khe/dot_general | solution.py:102
  395.9 17.5 %bitcast_add_fusion.5 = f32[1024,16,64]{0,2,1:T(8,128)} fusion(f32[1024,16,64]{0,2,1:T(8,128)} %get-tuple-element.427, f32[16,512,1024]{2,1,0:T(8,128)} %fusion.164, f32[16,512]{1,0:T(8,128)S(1)} %dynamic-slice_bitcast_fusion.2, pred[512,1024]{1,0:T(8,128)(4,1)S(1)} %fusion.165, pred[]{:T(512)S(6)} %compare.3, ...), kind=kOutput, calls=%fused_computation.25.clone.1 | convolution fusion | flops 1109393408 | bytes 43548676 | tf_op jit(solution)/shard_map/while/body/eval_jaxpr/hqk,qhe->khe/dot_general | solution.py:88
  413.5 9.8 %fusion.166 = bf16[2,512,16,64]{1,3,2,0:T(8,128)(2,1)} fusion(bf16[2,512,16,64]{1,3,2,0:T(8,128)(2,1)} %get-tuple-element.428, s32[]{:T(128)S(6)} %copy.80, bf16[16,512,1024]{2,1,0:T(8,128)(2,1)} %multiply_convert_fusion.7, bf16[1024,16,64]{0,2,1:T(8,128)(2,1)S(1)} %get-tuple-element.448), kind=kOutput, calls=%fused_computation.32.clone.1 | convolution fusion | flops 1074790400 | bytes 19922948 | tf_op jit(solution)/shard_map/while/body/eval_jaxpr/hqk,khe->qhe/dot_general | solution.py:97
  424.5 14.4 %fusion.164 = f32[16,512,1024]{2,1,0:T(8,128)} fusion(bf16[1024,16,64]{0,2,1:T(8,128)(2,1)S(1)} %get-tuple-element.448, bf16[1024,16,64]{0,2,1:T(8,128)(2,1)} %get-tuple-element.446, s32[]{:T(128)S(6)} %select_n.64), kind=kOutput, calls=%fused_computation.37.clone.1 | convolution fusion | flops 1073741824 | bytes 36700164 | tf_op jit(solution)/shard_map/while/body/eval_jaxpr/qhe,khe->hqk/dot_general | solution.py:47
  440.8 0.8 dynamic_slice.64
  442.2 26.0 %multiply_reduce_fusion.4 = (f32[16,512]{1,0:T(8,128)S(1)}, f32[16,512,1024]{2,1,0:T(8,128)}) fusion(f32[16,512,1024]{2,1,0:T(8,128)} %fusion.164, f32[16,512]{1,0:T(8,128)S(1)} %dynamic-slice_bitcast_fusion.2, pred[512,1024]{1,0:T(8,128)(4,1)S(1)} %fusion.165, bf16[1024,16,64]{0,2,1:T(8,128)(2,1)} %get-tuple-element.451, ...), kind=kOutput, calls=%fused_computation.20.clone.1 | convolution fusion | flops 1115676672 | bytes 70844416 | tf_op jit(solution)/shard_map/while/body/eval_jaxpr/qhe,khe->hqk/dot_general | solution.py:85
  468.1 27.8 %multiply_convert_fusion.7 = bf16[16,512,1024]{2,1,0:T(8,128)(2,1)} fusion(f32[16,512,1024]{2,1,0:T(8,128)} %get-tuple-element.371, f32[16,512,1024]{2,1,0:T(8,128)} %fusion.164, f32[16,512]{1,0:T(8,128)S(1)} %get-tuple-element.372, f32[16,512]{1,0:T(8,128)S(1)} %dynamic-slice_bitcast_fusion.2, pred[512,1024]{1,0:T(8,128)(4,1)S(1)} %fusion.165), kind=kLoop, calls=%fused_computation.19.clone.1 | loop fusion | flops 50331648 | bytes 84475904 | tf_op jit(solution)/shard_map/while/body/eval_jaxpr/convert_element_type | solution.py:95
  495.9 12.3 %bitcast_add_fusion.4 = f32[1024,16,64]{0,2,1:T(8,128)} fusion(f32[1024,16,64]{0,2,1:T(8,128)} %get-tuple-element.426, bf16[16,512,1024]{2,1,0:T(8,128)(2,1)} %multiply_convert_fusion.7, pred[]{:T(512)S(6)} %compare.3, bf16[1024,16,64]{0,2,1:T(8,128)(2,1)} %get-tuple-element.446, s32[]{:T(128)S(6)} %select_n.64), kind=kOutput, calls=%fused_computation.26.clone.1 | convolution fusion | flops 1076887552 | bytes 26214404 | tf_op jit(solution)/shard_map/while/body/eval_jaxpr/hqk,qhe->khe/dot_general | solution.py:102
  508.2 18.7 %bitcast_add_fusion.5 = f32[1024,16,64]{0,2,1:T(8,128)} fusion(f32[1024,16,64]{0,2,1:T(8,128)} %get-tuple-element.427, f32[16,512,1024]{2,1,0:T(8,128)} %fusion.164, f32[16,512]{1,0:T(8,128)S(1)} %dynamic-slice_bitcast_fusion.2, pred[512,1024]{1,0:T(8,128)(4,1)S(1)} %fusion.165, pred[]{:T(512)S(6)} %compare.3, ...), kind=kOutput, calls=%fused_computation.25.clone.1 | convolution fusion | flops 1109393408 | bytes 43548676 | tf_op jit(solution)/shard_map/while/body/eval_jaxpr/hqk,qhe->khe/dot_general | solution.py:88
  526.9 9.8 %fusion.166 = bf16[2,512,16,64]{1,3,2,0:T(8,128)(2,1)} fusion(bf16[2,512,16,64]{1,3,2,0:T(8,128)(2,1)} %get-tuple-element.428, s32[]{:T(128)S(6)} %copy.80, bf16[16,512,1024]{2,1,0:T(8,128)(2,1)} %multiply_convert_fusion.7, bf16[1024,16,64]{0,2,1:T(8,128)(2,1)S(1)} %get-tuple-element.448), kind=kOutput, calls=%fused_computation.32.clone.1 | convolution fusion | flops 1074790400 | bytes 19922948 | tf_op jit(solution)/shard_map/while/body/eval_jaxpr/hqk,khe->qhe/dot_general | solution.py:97
  536.9 2.7 convert_element_type.94
  540.6 2.2 copy.56
  546.5 17.0 %add_convert_fusion = bf16[1024,1024]{0,1:T(8,128)(2,1)} fusion(f32[1024,1024]{0,1:T(8,128)} %copy-done.8, f32[1024]{0:T(1024)S(1)} %bitcast.156, bf16[4096,1024]{1,0:T(8,128)(2,1)} %all-gather.13.cloned.1.call-done, f32[1024,4096]{1,0:T(8,128)} %fusion.63, f32[4096]{0:T(1024)S(1)} %copy-done.50), kind=kOutput, calls=%fused_computation.91 | convolution fusion | flops 8635023360 | bytes 31477760 | tf_op jit(solution)/shard_map/dot_general | solution.py:189
  563.5 4.1 copy.57
  567.6 2.7 convert_element_type.93
  570.3 0.8 fusion.77
  571.1 9.6 %fusion.42 = f32[1024,1024]{0,1:T(8,128)S(1)} fusion(bf16[1024,3072]{1,0:T(8,128)(2,1)} %all-gather.7.cloned.1.call-done, bf16[1024,1024]{0,1:T(8,128)(2,1)S(1)} %bitcast.140, bf16[1024,1024]{0,1:T(8,128)(2,1)S(1)} %bitcast.147, bf16[1024,1024]{0,1:T(8,128)(2,1)S(1)} %bitcast.143), kind=kOutput, calls=%fused_computation.60 | convolution fusion | flops 6461325312 | bytes 16777216 | tf_op jit(solution)/shard_map/dot_general | solution.py:14
  580.8 1.5 fusion.56
  582.3 1.0 fusion.69
  583.4 1.1 copy-done.10
  585.1 3.6 add_add_fusion.2
  588.8 5.4 copy.58
  594.2 7.2 %all-gather.15.cloned.1.call-done = f32[128,1024,4]{1,2,0:T(4,128)} async-done(((f32[4,1024,4]{1,2,0:T(4,128)}), f32[128,1024,4]{1,2,0:T(4,128)}) %all-gather.15.cloned.1.call-update) | async-done | bytes 2097168 | tf_op jit(solution)/shard_map/all_gather | solution.py:239
  601.4 2.1 reduce_sum.123
  (168 shorter events, 19.4 us)
Async XLA Ops:
  7.2 5.8 copy-start.42
  7.2 6.4 %copy-start.43 = (f32[2,1024]{1,0:T(2,128)S(1)}, f32[2,1024]{1,0:T(2,128)}, u32[]{:S(2)}) copy-start(f32[2,1024]{1,0:T(2,128)} %param.22) | copy-start | bytes 24580
  7.2 67.5 %all-gather.7.cloned.1.call-start = ((), (), s32[]{:S(2)}) async-start(), calls=%async_computation | async-start | bytes 6684672 | tf_op jit(solution)/shard_map/all_gather | solution.py:140
  7.9 203.0 %all-gather.9.cloned.1.call-start = ((), (), s32[]{:S(2)}) async-start(), calls=%async_computation.1 | async-start | bytes 2228224 | tf_op jit(solution)/shard_map/all_gather | solution.py:141
  8.7 210.5 %all-gather.11.cloned.1.call-start = ((), (), s32[]{:S(2)}) async-start(), calls=%async_computation.2 | async-start | bytes 8912896 | tf_op jit(solution)/shard_map/all_gather | solution.py:144
  9.4 258.5 %all-gather.13.cloned.1.call-start = ((), (), s32[]{:S(2)}) async-start(), calls=%async_computation.3 | async-start | bytes 8912896 | tf_op jit(solution)/shard_map/all_gather | solution.py:145
  10.0 591.4 %all-gather.15.cloned.1.call-start = ((), (), s32[]{:S(2)}) async-start(), calls=%async_computation.4 | async-start | bytes 2162688 | tf_op jit(solution)/shard_map/all_gather | solution.py:239
  10.0 5.8 copy-start.23
  13.0 3.7 copy-start.1
  14.3 2.4 copy-start.37
  14.6 2.5 copy-start.25
  15.2 0.6 copy-start.35
  15.8 1.3 copy-start.33
  15.9 79.2 %copy-start.19 = (bf16[4,1024,4]{1,2,0:T(4,128)(2,1)}, bf16[4,1024,4]{1,2,0:T(4,128)(2,1)S(1)}, u32[]{:S(2)}) copy-start(bf16[4,1024,4]{1,2,0:T(4,128)(2,1)S(1)} %convert_element_type.81) | copy-start | bytes 98308
  15.9 2.6 copy-start.44
  16.7 1.3 copy-start.3
  16.7 58.0 %copy-start.51 = (f32[3072]{0:T(1024)S(1)}, f32[3072]{0:T(1024)}, u32[]{:S(2)}) copy-start(f32[3072]{0:T(1024)} %param.25) | copy-start | bytes 36868
  18.0 67.5 %copy-start.27 = (bf16[1024,4]{0,1:T(4,128)(2,1)}, bf16[1024,4]{0,1:T(4,128)(2,1)S(1)}, u32[]{:S(2)}) copy-start(bf16[1024,4]{0,1:T(4,128)(2,1)S(1)} %convolution_convert_fusion.1) | copy-start | bytes 24580
  18.4 76.6 %copy-start.29 = (bf16[1024,4]{0,1:T(4,128)(2,1)}, bf16[1024,4]{0,1:T(4,128)(2,1)S(1)}, u32[]{:S(2)}) copy-start(bf16[1024,4]{0,1:T(4,128)(2,1)S(1)} %convolution_convert_fusion) | copy-start | bytes 24580
  18.4 56.3 %copy-start.4 = (bf16[1024,1024]{0,1:T(8,128)(2,1)S(1)}, bf16[1024,1024]{0,1:T(8,128)(2,1)}, u32[]{:S(2)}) copy-start(bf16[1024,1024]{0,1:T(8,128)(2,1)} %copy-done.3) | copy-start | bytes 6291460
  83.7 5.2 copy-start.11
  123.2 15.9 %copy-start = (bf16[1024,16,64]{0,2,1:T(8,128)(2,1)S(1)}, bf16[1024,16,64]{0,2,1:T(8,128)(2,1)}, u32[]{:S(2)}) copy-start(bf16[1024,16,64]{0,2,1:T(8,128)(2,1)} %get-tuple-element.404) | copy-start | bytes 6291460 | tf_op jit(solution)/shard_map/while
  123.2 15.9 %copy-start.13 = (bf16[2,512,16,64]{1,3,2,0:T(8,128)(2,1)S(1)}, bf16[2,512,16,64]{1,3,2,0:T(8,128)(2,1)}, u32[]{:S(2)}) copy-start(bf16[2,512,16,64]{1,3,2,0:T(8,128)(2,1)} %get-tuple-element.386) | copy-start | bytes 6291460 | tf_op jit(solution)/shard_map/while
  153.8 1.3 copy-start.14
  173.1 15.7 %copy-start = (bf16[1024,16,64]{0,2,1:T(8,128)(2,1)S(1)}, bf16[1024,16,64]{0,2,1:T(8,128)(2,1)}, u32[]{:S(2)}) copy-start(bf16[1024,16,64]{0,2,1:T(8,128)(2,1)} %get-tuple-element.404) | copy-start | bytes 6291460 | tf_op jit(solution)/shard_map/while
  173.2 15.7 %copy-start.13 = (bf16[2,512,16,64]{1,3,2,0:T(8,128)(2,1)S(1)}, bf16[2,512,16,64]{1,3,2,0:T(8,128)(2,1)}, u32[]{:S(2)}) copy-start(bf16[2,512,16,64]{1,3,2,0:T(8,128)(2,1)} %get-tuple-element.386) | copy-start | bytes 6291460 | tf_op jit(solution)/shard_map/while
  203.7 1.3 copy-start.14
  205.2 5.7 copy-start.47
  216.6 2.0 copy-start.8
  216.6 2.5 copy-start.39
  216.7 2.5 copy-start.46
  219.2 48.8 %copy-start.49 = (f32[4096]{0:T(1024)S(1)}, f32[4096]{0:T(1024)}, u32[]{:S(2)}) copy-start(f32[4096]{0:T(1024)} %param.28) | copy-start | bytes 49156
  301.6 4.7 copy-start.15
  301.7 4.7 copy-start.48
  306.3 3.8 copy-start.9
  306.4 3.8 copy-start.40
  312.1 17.5 %copy-start.17 = (f32[2,16,512]{2,1,0:T(8,128)}, f32[2,16,512]{2,1,0:T(8,128)S(1)}, u32[]{:S(2)}) copy-start(f32[2,16,512]{2,1,0:T(8,128)S(1)} %get-tuple-element.449) | copy-start | bytes 196612 | tf_op jit(solution)/shard_map/while
  413.5 9.8 %copy-start.18 = (f32[2,16,512]{2,1,0:T(8,128)S(1)}, f32[2,16,512]{2,1,0:T(8,128)}, u32[]{:S(2)}) copy-start(f32[2,16,512]{2,1,0:T(8,128)} %copy-done.17) | copy-start | bytes 196612 | tf_op jit(solution)/shard_map/while
  423.2 17.5 %copy-start.17 = (f32[2,16,512]{2,1,0:T(8,128)}, f32[2,16,512]{2,1,0:T(8,128)S(1)}, u32[]{:S(2)}) copy-start(f32[2,16,512]{2,1,0:T(8,128)S(1)} %get-tuple-element.449) | copy-start | bytes 196612 | tf_op jit(solution)/shard_map/while
  526.9 9.8 %copy-start.18 = (f32[2,16,512]{2,1,0:T(8,128)S(1)}, f32[2,16,512]{2,1,0:T(8,128)}, u32[]{:S(2)}) copy-start(f32[2,16,512]{2,1,0:T(8,128)} %copy-done.17) | copy-start | bytes 196612 | tf_op jit(solution)/shard_map/while
  536.9 2.7 copy-start.20
  536.9 3.1 copy-start.30
  536.9 3.7 copy-start.12
  542.8 1.0 copy-start.28
  542.8 1.7 copy-start.5
  543.4 2.4 copy-start.6
  543.4 3.1 copy-start.45
  543.4 3.1 copy-start.50
  567.6 3.4 copy-start.7
  571.1 9.7 %copy-start.2 = (bf16[1024,1024]{0,1:T(8,128)(2,1)S(1)}, bf16[1024,1024]{0,1:T(8,128)(2,1)}, u32[]{:S(2)}) copy-start(bf16[1024,1024]{0,1:T(8,128)(2,1)} %copy-done.1) | copy-start | bytes 6291460
  571.1 9.7 %copy-start.26 = (f32[1024]{0:T(1024)S(1)}, f32[1024]{0:T(1024)}, u32[]{:S(2)}) copy-start(f32[1024]{0:T(1024)} %copy-done.25) | copy-start | bytes 12292
  571.1 9.7 %copy-start.38 = (f32[1,1024]{1,0:T(1,128)S(1)}, f32[1,1024]{1,0:T(1,128)}, u32[]{:S(2)}) copy-start(f32[1,1024]{1,0:T(1,128)} %copy-done.37) | copy-start | bytes 12292
  580.8 1.6 copy-start.36
  580.8 1.6 copy-start.34
  582.3 2.2 copy-start.10
  582.3 2.9 copy-start.16
  582.3 2.9 copy-start.41
  588.8 14.7 %copy-start.24 = (f32[4,1024,4]{1,2,0:T(4,128)S(1)}, f32[4,1024,4]{1,2,0:T(4,128)}, u32[]{:S(2)}) copy-start(f32[4,1024,4]{1,2,0:T(4,128)} %param.31) | copy-start | bytes 196612
  588.8 14.7 %copy-start.32 = (f32[4,1024,4]{1,2,0:T(4,128)S(1)}, f32[4,1024,4]{1,2,0:T(4,128)}, u32[]{:S(2)}) copy-start(f32[4,1024,4]{1,2,0:T(4,128)} %param.32) | copy-start | bytes 196612
  588.8 15.4 %copy-start.31 = (f32[4,1024,4]{1,2,0:T(4,128)S(1)}, f32[4,1024,4]{1,2,0:T(4,128)}, u32[]{:S(2)}) copy-start(f32[4,1024,4]{1,2,0:T(4,128)} %param.33) | copy-start | bytes 196612
  603.5 1.4 copy-start.21
  604.2 0.7 copy-start.22
Sparse Core Ops, SparseCore 0:
  10.3 64.3 all-gather.6
  76.9 39.9 all-gather.8
  119.0 73.6 all-gather.10
  194.8 73.1 all-gather.12
  546.6 54.7 all-gather.14
